TPU v7x, 32 devices: a whole 2x2x4 slice. The times are simulated.
32 devices in a mesh: gx: 2 (over x), gy: 4 (over z), gz: 4 (over y, core).
Axes of the slice: x: 2, y: 2, z: 4, core: 2. Of those that a mesh axis runs over, the one named last changes fastest.
Arguments:
- local_displacement: float32 [2, 4, 4, 6, 128, 128], P('gx', 'gy', 'gz'), may hold values from -6 to 6
- coarse_load: float32 [2, 4, 4, 6, 128], P('gx', 'gy', 'gz'), may hold values from -12 to 12
- flexibility: float32 [2, 4, 4, 768, 768], P('gx', 'gy', 'gz'), as said below
- block_map: int32 [2, 4, 4, 768], P('gx', 'gy', 'gz'), may hold values from 0 to 767, each once within a row
- mode_counts: int32 [2, 4, 4], P('gx', 'gy', 'gz'), may hold values from 3 to 6, as said below
- mode_traces: float32 [2, 4, 4, 6, 6, 128], P('gx', 'gy', 'gz')
- coarse_rows: float32 [2, 4, 4, 6, 192], P('gx', 'gy', 'gz'), as said below
- stored_dirs: float32 [2, 4, 4, 40, 6, 128], P('gx', 'gy', 'gz'), as said below
- stored_images: float32 [2, 4, 4, 40, 6, 128], P('gx', 'gy', 'gz'), as said below
- stored_curv: float32 [40], replicated, may hold values from 1 to 4
Outputs:
- multipliers: float32 [2, 4, 4, 6, 128, 128], P('gx', 'gy', 'gz')
- residual: float32 [2, 4, 4, 6, 128, 128], P('gx', 'gy', 'gz')
Inputs may be any that keep to these rules, and one draw needn't show every extreme that they name: `flexibility`: each subdomain's matrix is symmetric positive definite. `coarse_rows`: read as a [192, 192] matrix it is exactly symmetric: the inverse of G^T G for the coarse basis G of the present modes, with ones added on the diagonal of absent modes. `mode_counts`: modes numbered from the count on are absent. `block_map`: each subdomain's row names every interface position once. `stored_dirs`: both copies of every face agree: slot 2a of a subdomain equals slot 2a+1 of its lower neighbour along grid dimension a. `stored_images`: both copies of every face agree: slot 2a of a subdomain equals slot 2a+1 of its lower neighbour along grid dimension a.
All inputs are finite; a program needn't handle non-finite values.
Results may differ from a plain program's by a relative error of at most 0.0003.
Values sent between devices are 32-bit elements; how exact they have to be, the bound alone decides.
A program may use at most 128 MiB of HBM per device.

v0:
```python
import jax
import jax.numpy as jnp
from jax import lax
from jax.sharding import PartitionSpec as P

STORED = 40
ITERS = 3
precise = lax.Precision.HIGHEST
slot_signs = (-1.0, 1.0, -1.0, 1.0, -1.0, 1.0)


def extended(x, sides, width):
    for axis, dim in sides:
        peers, length = (lax.axis_size(axis), x.shape[dim])
        up = [(i, (i + 1) % peers) for i in range(peers)]
        down = [(j, i) for i, j in up]
        last = lax.slice_in_dim(x, length - width, length, axis=dim)
        initial = lax.slice_in_dim(x, 0, width, axis=dim)
        before = lax.ppermute(last, axis, up)
        after = lax.ppermute(initial, axis, down)
        x = jnp.concatenate([before, x, after], axis=dim)
    return x


def assemble(field):
    padded_x = extended(field[0:2], (("gx", 0),), 1)
    padded_y = extended(field[2:4], (("gy", 0),), 1)
    padded_z = extended(field[4:6], (("gz", 0),), 1)
    return jnp.stack(
        [
            field[0] + padded_x[0],
            field[1] + padded_x[3],
            field[2] + padded_y[0],
            field[3] + padded_y[3],
            field[4] + padded_z[0],
            field[5] + padded_z[3],
        ]
    )


def plus_inner(first, second):
    return jnp.sum(first[1::2] * second[1::2], axis=(0, 1))


def stored_inner(store, field):
    return jnp.einsum("isf,sfr->ir", store[:, 1::2], field[1::2], precision=precise)


def coarse_solve(loads, rows):
    return jnp.dot(
        rows, lax.all_gather(loads, ("gx", "gy", "gz"), axis=0, tiled=True), precision=precise
    )


def per_device(
    local_displacement,
    coarse_load,
    flexibility,
    block_map,
    mode_counts,
    mode_traces,
    coarse_rows,
    stored_dirs,
    stored_images,
    stored_curv,
):
    displacement = local_displacement[0, 0, 0]
    loads = coarse_load[0, 0, 0]
    flex = flexibility[0, 0, 0]
    mapping = block_map[0, 0, 0]
    rows = coarse_rows[0, 0, 0]
    dirs_store = stored_dirs[0, 0, 0]
    images_store = stored_images[0, 0, 0]
    signs = jnp.array(slot_signs, jnp.float32)
    field_signs = signs[:, None, None]
    nmodes = mode_traces.shape[3]
    present = (jnp.arange(nmodes, dtype=jnp.int32) < mode_counts[0, 0, 0]).astype(jnp.float32)
    signed = mode_traces[0, 0, 0] * present[:, None, None] * signs[None, :, None]
    size_nb = flex.shape[0]
    inverse = jnp.zeros((size_nb,), jnp.int32).at[mapping].set(jnp.arange(size_nb, dtype=jnp.int32))
    flex_face = jnp.take(jnp.take(flex, inverse, axis=0), inverse, axis=1)
    layout = displacement.shape

    def operate(field):
        flat = (field_signs * field).reshape(size_nb, layout[2])
        return jnp.dot(flex_face, flat, precision=precise).reshape(layout)

    def graph(alpha):
        return assemble(jnp.einsum("msf,mr->sfr", signed, alpha, precision=precise))

    def project(field):
        partial_loads = jnp.einsum("msf,sfr->mr", signed, field, precision=precise)
        return field - graph(coarse_solve(partial_loads, rows))

    lam = graph(coarse_solve(loads, rows))
    resid = project(assemble(field_signs * (displacement - operate(lam))))
    directions, images, curves = ([], [], [])
    for step in range(ITERS):
        local_rows = stored_inner(images_store, resid)
        if images:
            own_rows = jnp.stack([plus_inner(images[index], resid) for index in range(len(images))])
            local_rows = jnp.concatenate([local_rows, own_rows], axis=0)
        totals = lax.psum(local_rows, ("gx", "gy", "gz"))
        beta = totals[:STORED] / stored_curv[:, None]
        direction = resid - jnp.einsum("isf,ir->sfr", dirs_store, beta, precision=precise)
        for index in range(len(directions)):
            direction = direction - directions[index] * (totals[STORED + index] / curves[index])
        image_now = project(assemble(field_signs * operate(direction)))
        pair = lax.psum(
            jnp.stack([plus_inner(direction, image_now), plus_inner(direction, resid)]),
            ("gx", "gy", "gz"),
        )
        rate = pair[1] / pair[0]
        lam = lam + rate * direction
        resid = resid - rate * image_now
        directions.append(direction)
        images.append(image_now)
        curves.append(pair[0])
    return (lam[None, None, None], resid[None, None, None])


def solution(mesh):
    return jax.shard_map(
        per_device,
        mesh=mesh,
        in_specs=(
            P("gx", "gy", "gz", None, None, None),
            P("gx", "gy", "gz", None, None),
            P("gx", "gy", "gz", None, None),
            P("gx", "gy", "gz", None),
            P("gx", "gy", "gz"),
            P("gx", "gy", "gz", None, None, None),
            P("gx", "gy", "gz", None, None),
            P("gx", "gy", "gz", None, None, None),
            P("gx", "gy", "gz", None, None, None),
            P(),
        ),
        out_specs=(P("gx", "gy", "gz", None, None, None), P("gx", "gy", "gz", None, None, None)),
        check_vma=False,
    )
```

profile of v0, /device:TPU:10, one launch (start us, length us, event | category | flops | bytes accessed | tf_op | source)
XLA Modules:
  0.0 665.6 jit_solution(9631356648595068276)
XLA Ops:
  1.5 37.6 %all-gather = f32[1,1,1,192,128]{4,2,1,0,3:T(1,128)S(1)} all-gather(f32[1,1,1,6,128]{4,2,1,0,3:T(1,128)} %bitcast.275), channel_id=2, replica_groups=mesh['gx'=2,'gy'=4,'gz'=4] {'gx','gy','gz'}, dimensions={3}, use_global_device_ids=true | all-gather | bytes 101376 | tf_op jit(solution)/shard_map/all_gather | solution.py:51
  43.9 3.4 scatter_custom_fusion
  47.3 3.5 gather_fusion
  57.1 5.8 gather_fusion.1
  71.2 4.2 collective-permute-start.3
  78.9 3.7 fusion.4
  87.5 4.6 collective-permute-start.8
  99.1 37.6 %all-gather.1 = f32[32,6,128]{2,1,0:T(8,128)S(1)} all-gather(f32[1,6,128]{2,1,0:T(8,128)S(1)} %convolution_bitcast_fusion.14), channel_id=1, replica_groups=mesh['gx'=2,'gy'=4,'gz'=4] {'gx','gy','gz'}, dimensions={0}, use_global_device_ids=true | all-gather | bytes 101376 | tf_op jit(solution)/shard_map/all_gather | solution.py:51
  142.8 4.2 collective-permute-start.15
  153.1 43.5 %psum.42 = f32[40,128]{1,0:T(8,128)} all-reduce(f32[40,128]{1,0:T(8,128)S(1)} %convolution_bitcast_fusion.5), channel_id=1, replica_groups=mesh['gx'=2,'gy'=4,'gz'=4] {'gx','gy','gz'}, use_global_device_ids=true, to_apply=%region_1.2 | all-reduce | flops 5120 | bytes 40960 | tf_op jit(solution)/shard_map/psum | solution.py:103
  198.4 3.7 convolution_multiply_fusion.2
  202.4 4.1 collective-permute-done.18
  209.7 3.6 collective-permute-done.19
  214.1 39.5 %all-gather.2 = f32[32,6,128]{2,1,0:T(8,128)} all-gather(f32[1,6,128]{2,1,0:T(8,128)S(1)} %convolution_bitcast_fusion.13), channel_id=1, replica_groups=mesh['gx'=2,'gy'=4,'gz'=4] {'gx','gy','gz'}, dimensions={0}, use_global_device_ids=true | all-gather | bytes 101376 | tf_op jit(solution)/shard_map/all_gather | solution.py:51
  267.2 4.2 collective-permute-start.27
  272.8 3.4 collective-permute-done.25
  278.5 42.5 %psum.43 = f32[2,128]{1,0:T(2,128)S(1)} all-reduce(f32[2,128]{1,0:T(2,128)S(1)} %pad_maximum_fusion.2), channel_id=1, replica_groups=mesh['gx'=2,'gy'=4,'gz'=4] {'gx','gy','gz'}, use_global_device_ids=true, to_apply=%region_4.5 | all-reduce | flops 256 | bytes 2048 | tf_op jit(solution)/shard_map/psum | solution.py:109
  324.6 39.2 %psum.44 = f32[41,128]{1,0:T(8,128)S(1)} all-reduce(f32[41,128]{1,0:T(8,128)S(1)} %pad_maximum_fusion), channel_id=1, replica_groups=mesh['gx'=2,'gy'=4,'gz'=4] {'gx','gy','gz'}, use_global_device_ids=true, to_apply=%region_6.7 | all-reduce | flops 5248 | bytes 41984 | tf_op jit(solution)/shard_map/psum | solution.py:103
  367.1 3.7 convolution_multiply_fusion.1
  371.0 4.1 collective-permute-done.30
  378.5 3.9 collective-permute-done.31
  383.3 38.7 %all-gather.3 = f32[32,6,128]{2,1,0:T(8,128)S(1)} all-gather(f32[1,6,128]{2,1,0:T(8,128)S(1)} %convolution_bitcast_fusion.12), channel_id=1, replica_groups=mesh['gx'=2,'gy'=4,'gz'=4] {'gx','gy','gz'}, dimensions={0}, use_global_device_ids=true | all-gather | bytes 101376 | tf_op jit(solution)/shard_map/all_gather | solution.py:51
  433.3 4.2 collective-permute-start.39
  438.8 3.6 collective-permute-done.37
  445.1 42.5 %psum.45 = f32[2,128]{1,0:T(2,128)} all-reduce(f32[2,128]{1,0:T(2,128)} %pad_maximum_fusion.3), channel_id=1, replica_groups=mesh['gx'=2,'gy'=4,'gz'=4] {'gx','gy','gz'}, use_global_device_ids=true, to_apply=%region_9.10 | all-reduce | flops 256 | bytes 2048 | tf_op jit(solution)/shard_map/psum | solution.py:109
  491.8 39.6 %psum.46 = f32[42,128]{1,0:T(8,128)S(1)} all-reduce(f32[42,128]{1,0:T(8,128)S(1)} %pad_maximum_fusion.1), channel_id=1, replica_groups=mesh['gx'=2,'gy'=4,'gz'=4] {'gx','gy','gz'}, use_global_device_ids=true, to_apply=%region_12.13 | all-reduce | flops 5376 | bytes 43008 | tf_op jit(solution)/shard_map/psum | solution.py:103
  534.9 3.7 convolution_multiply_fusion
  538.9 4.1 collective-permute-done.42
  546.3 3.6 collective-permute-done.43
  550.9 38.9 %all-gather.4 = f32[32,6,128]{2,1,0:T(8,128)S(1)} all-gather(f32[1,6,128]{2,1,0:T(8,128)S(1)} %convolution_bitcast_fusion.11), channel_id=1, replica_groups=mesh['gx'=2,'gy'=4,'gz'=4] {'gx','gy','gz'}, dimensions={0}, use_global_device_ids=true | all-gather | bytes 101376 | tf_op jit(solution)/shard_map/all_gather | solution.py:51
  601.0 4.2 collective-permute-start.51
  611.6 42.5 %psum.47 = f32[2,128]{1,0:T(2,128)S(1)} all-reduce(f32[2,128]{1,0:T(2,128)S(1)} %pad_maximum_fusion.4), channel_id=1, replica_groups=mesh['gx'=2,'gy'=4,'gz'=4] {'gx','gy','gz'}, use_global_device_ids=true, to_apply=%region_15.16 | all-reduce | flops 256 | bytes 2048 | tf_op jit(solution)/shard_map/psum | solution.py:109
  (456 shorter events, 137.0 us)
Async XLA Ops:
  41.6 21.3 %collective-permute-start = (f32[1,128,128]{2,1,0:T(8,128)S(1)}, f32[1,128,128]{2,1,0:T(8,128)}, u32[]{:S(2)}, u32[]{:S(2)}) collective-permute-start(f32[1,128,128]{2,1,0:T(8,128)S(1)} %slice.456), channel_id=1, source_target_pairs={{0,16},{16,0},{1,17},{17,1},{2,18},{18,2},{3,19},{19,3},{4,20},{20... | collective-permute-start | bytes 196616 | tf_op jit(solution)/shard_map/ppermute | solution.py:19
  63.7 11.7 %collective-permute-start.1 = (f32[1,128,128]{2,1,0:T(8,128)S(1)}, f32[1,128,128]{2,1,0:T(8,128)}, u32[]{:S(2)}, u32[]{:S(2)}) collective-permute-start(f32[1,128,128]{2,1,0:T(8,128)S(1)} %get-tuple-element.63), channel_id=1, source_target_pairs={{16,0},{0,16},{17,1},{1,17},{18,2},{2,18},{19,3},{3,19},{20,4},{4,... | collective-permute-start | bytes 196616 | tf_op jit(solution)/shard_map/ppermute | solution.py:20
  70.7 7.4 %collective-permute-start.5 = (f32[1,128,128]{2,1,0:T(8,128)S(1)}, f32[1,128,128]{2,1,0:T(8,128)S(1)}, u32[]{:S(2)}, u32[]{:S(2)}) collective-permute-start(f32[1,128,128]{2,1,0:T(8,128)S(1)} %get-tuple-element.58), channel_id=1, source_target_pairs={{1,0},{2,1},{3,2},{0,3},{5,4},{6,5},{7,6},{4,7},{9,8},{10,9},{11,1... | collective-permute-start | bytes 196616 | tf_op jit(solution)/shard_map/ppermute | solution.py:20
  70.7 7.3 %collective-permute-start.4 = (f32[1,128,128]{2,1,0:T(8,128)S(1)}, f32[1,128,128]{2,1,0:T(8,128)S(1)}, u32[]{:S(2)}, u32[]{:S(2)}) collective-permute-start(f32[1,128,128]{2,1,0:T(8,128)S(1)} %get-tuple-element.60), channel_id=1, source_target_pairs={{0,1},{1,2},{2,3},{3,0},{4,5},{5,6},{6,7},{7,4},{8,9},{9,10},{10,1... | collective-permute-start | bytes 196616 | tf_op jit(solution)/shard_map/ppermute | solution.py:19
  87.0 11.1 %collective-permute-start.11 = (f32[1,128,128]{2,1,0:T(8,128)S(1)}, f32[1,128,128]{2,1,0:T(8,128)S(1)}, u32[]{:S(2)}, u32[]{:S(2)}) collective-permute-start(f32[1,128,128]{2,1,0:T(8,128)S(1)} %get-tuple-element.52), channel_id=1, source_target_pairs={{1,0},{2,1},{3,2},{0,3},{5,4},{6,5},{7,6},{4,7},{9,8},{10,9},{11,1... | collective-permute-start | bytes 196616 | tf_op jit(solution)/shard_map/ppermute | solution.py:20
  87.0 11.0 %collective-permute-start.10 = (f32[1,128,128]{2,1,0:T(8,128)S(1)}, f32[1,128,128]{2,1,0:T(8,128)S(1)}, u32[]{:S(2)}, u32[]{:S(2)}) collective-permute-start(f32[1,128,128]{2,1,0:T(8,128)S(1)} %get-tuple-element.54), channel_id=1, source_target_pairs={{0,1},{1,2},{2,3},{3,0},{4,5},{5,6},{6,7},{7,4},{8,9},{9,10},{10,1... | collective-permute-start | bytes 196616 | tf_op jit(solution)/shard_map/ppermute | solution.py:19
  87.5 8.9 %collective-permute-start.8 = (f32[1,128,128]{2,1,0:T(8,128)S(1)}, f32[1,128,128]{2,1,0:T(8,128)S(1)}, u32[]{:S(2)}, u32[]{:S(2)}) collective-permute-start(f32[1,128,128]{2,1,0:T(8,128)S(1)} %get-tuple-element.55), channel_id=1, source_target_pairs={{0,4},{4,8},{8,12},{12,0},{1,5},{5,9},{9,13},{13,1},{2,6},{6,10},{... | collective-permute-start | bytes 196616 | tf_op jit(solution)/shard_map/ppermute | solution.py:19
  142.2 9.3 %collective-permute-start.17 = (f32[1,128,128]{2,1,0:T(8,128)S(1)}, f32[1,128,128]{2,1,0:T(8,128)S(1)}, u32[]{:S(2)}, u32[]{:S(2)}) collective-permute-start(f32[1,128,128]{2,1,0:T(8,128)S(1)} %get-tuple-element.46), channel_id=1, source_target_pairs={{1,0},{2,1},{3,2},{0,3},{5,4},{6,5},{7,6},{4,7},{9,8},{10,9},{11,1... | collective-permute-start | bytes 196616 | tf_op jit(solution)/shard_map/ppermute | solution.py:20
  142.3 9.2 %collective-permute-start.16 = (f32[1,128,128]{2,1,0:T(8,128)S(1)}, f32[1,128,128]{2,1,0:T(8,128)S(1)}, u32[]{:S(2)}, u32[]{:S(2)}) collective-permute-start(f32[1,128,128]{2,1,0:T(8,128)S(1)} %get-tuple-element.48), channel_id=1, source_target_pairs={{0,1},{1,2},{2,3},{3,0},{4,5},{5,6},{6,7},{7,4},{8,9},{9,10},{10,1... | collective-permute-start | bytes 196616 | tf_op jit(solution)/shard_map/ppermute | solution.py:19
  142.8 8.6 %collective-permute-start.14 = (f32[1,128,128]{2,1,0:T(8,128)S(1)}, f32[1,128,128]{2,1,0:T(8,128)S(1)}, u32[]{:S(2)}, u32[]{:S(2)}) collective-permute-start(f32[1,128,128]{2,1,0:T(8,128)S(1)} %get-tuple-element.49), channel_id=1, source_target_pairs={{0,4},{4,8},{8,12},{12,0},{1,5},{5,9},{9,13},{13,1},{2,6},{6,10},{... | collective-permute-start | bytes 196616 | tf_op jit(solution)/shard_map/ppermute | solution.py:19
  142.8 8.7 %collective-permute-start.15 = (f32[1,128,128]{2,1,0:T(8,128)S(1)}, f32[1,128,128]{2,1,0:T(8,128)S(1)}, u32[]{:S(2)}, u32[]{:S(2)}) collective-permute-start(f32[1,128,128]{2,1,0:T(8,128)S(1)} %get-tuple-element.50), channel_id=1, source_target_pairs={{4,0},{8,4},{12,8},{0,12},{5,1},{9,5},{13,9},{1,13},{6,2},{10,6},{... | collective-permute-start | bytes 196616 | tf_op jit(solution)/shard_map/ppermute | solution.py:20
  206.5 7.0 %collective-permute-start.23 = (f32[1,128,128]{2,1,0:T(8,128)S(1)}, f32[1,128,128]{2,1,0:T(8,128)S(1)}, u32[]{:S(2)}, u32[]{:S(2)}) collective-permute-start(f32[1,128,128]{2,1,0:T(8,128)S(1)} %get-tuple-element.40), channel_id=1, source_target_pairs={{1,0},{2,1},{3,2},{0,3},{5,4},{6,5},{7,6},{4,7},{9,8},{10,9},{11,1... | collective-permute-start | bytes 196616 | tf_op jit(solution)/shard_map/ppermute | solution.py:20
  206.6 6.9 %collective-permute-start.22 = (f32[1,128,128]{2,1,0:T(8,128)S(1)}, f32[1,128,128]{2,1,0:T(8,128)S(1)}, u32[]{:S(2)}, u32[]{:S(2)}) collective-permute-start(f32[1,128,128]{2,1,0:T(8,128)S(1)} %get-tuple-element.42), channel_id=1, source_target_pairs={{0,1},{1,2},{2,3},{3,0},{4,5},{5,6},{6,7},{7,4},{8,9},{9,10},{10,1... | collective-permute-start | bytes 196616 | tf_op jit(solution)/shard_map/ppermute | solution.py:19
  257.8 8.7 %collective-permute-start.24 = (f32[1,128,128]{2,1,0:T(8,128)S(1)}, f32[1,128,128]{2,1,0:T(8,128)S(1)}, u32[]{:S(2)}, u32[]{:S(2)}) collective-permute-start(f32[1,128,128]{2,1,0:T(8,128)S(1)} %slice.480), channel_id=1, source_target_pairs={{0,16},{16,0},{1,17},{17,1},{2,18},{18,2},{3,19},{19,3},{4,20},{20... | collective-permute-start | bytes 196616 | tf_op jit(solution)/shard_map/ppermute | solution.py:19
  266.6 9.8 %collective-permute-start.29 = (f32[1,128,128]{2,1,0:T(8,128)S(1)}, f32[1,128,128]{2,1,0:T(8,128)S(1)}, u32[]{:S(2)}, u32[]{:S(2)}) collective-permute-start(f32[1,128,128]{2,1,0:T(8,128)S(1)} %get-tuple-element.34), channel_id=1, source_target_pairs={{1,0},{2,1},{3,2},{0,3},{5,4},{6,5},{7,6},{4,7},{9,8},{10,9},{11,1... | collective-permute-start | bytes 196616 | tf_op jit(solution)/shard_map/ppermute | solution.py:20
  266.7 9.7 %collective-permute-start.28 = (f32[1,128,128]{2,1,0:T(8,128)S(1)}, f32[1,128,128]{2,1,0:T(8,128)S(1)}, u32[]{:S(2)}, u32[]{:S(2)}) collective-permute-start(f32[1,128,128]{2,1,0:T(8,128)S(1)} %get-tuple-element.36), channel_id=1, source_target_pairs={{0,1},{1,2},{2,3},{3,0},{4,5},{5,6},{6,7},{7,4},{8,9},{9,10},{10,1... | collective-permute-start | bytes 196616 | tf_op jit(solution)/shard_map/ppermute | solution.py:19
  267.1 9.1 %collective-permute-start.26 = (f32[1,128,128]{2,1,0:T(8,128)S(1)}, f32[1,128,128]{2,1,0:T(8,128)S(1)}, u32[]{:S(2)}, u32[]{:S(2)}) collective-permute-start(f32[1,128,128]{2,1,0:T(8,128)S(1)} %get-tuple-element.37), channel_id=1, source_target_pairs={{0,4},{4,8},{8,12},{12,0},{1,5},{5,9},{9,13},{13,1},{2,6},{6,10},{... | collective-permute-start | bytes 196616 | tf_op jit(solution)/shard_map/ppermute | solution.py:19
  267.2 9.1 %collective-permute-start.27 = (f32[1,128,128]{2,1,0:T(8,128)S(1)}, f32[1,128,128]{2,1,0:T(8,128)S(1)}, u32[]{:S(2)}, u32[]{:S(2)}) collective-permute-start(f32[1,128,128]{2,1,0:T(8,128)S(1)} %get-tuple-element.38), channel_id=1, source_target_pairs={{4,0},{8,4},{12,8},{0,12},{5,1},{9,5},{13,9},{1,13},{6,2},{10,6},{... | collective-permute-start | bytes 196616 | tf_op jit(solution)/shard_map/ppermute | solution.py:20
  375.2 7.3 %collective-permute-start.35 = (f32[1,128,128]{2,1,0:T(8,128)S(1)}, f32[1,128,128]{2,1,0:T(8,128)S(1)}, u32[]{:S(2)}, u32[]{:S(2)}) collective-permute-start(f32[1,128,128]{2,1,0:T(8,128)S(1)} %get-tuple-element.28), channel_id=1, source_target_pairs={{1,0},{2,1},{3,2},{0,3},{5,4},{6,5},{7,6},{4,7},{9,8},{10,9},{11,1... | collective-permute-start | bytes 196616 | tf_op jit(solution)/shard_map/ppermute | solution.py:20
  375.2 7.2 %collective-permute-start.34 = (f32[1,128,128]{2,1,0:T(8,128)S(1)}, f32[1,128,128]{2,1,0:T(8,128)S(1)}, u32[]{:S(2)}, u32[]{:S(2)}) collective-permute-start(f32[1,128,128]{2,1,0:T(8,128)S(1)} %get-tuple-element.30), channel_id=1, source_target_pairs={{0,1},{1,2},{2,3},{3,0},{4,5},{5,6},{6,7},{7,4},{8,9},{9,10},{10,1... | collective-permute-start | bytes 196616 | tf_op jit(solution)/shard_map/ppermute | solution.py:19
  423.8 8.9 %collective-permute-start.36 = (f32[1,128,128]{2,1,0:T(8,128)S(1)}, f32[1,128,128]{2,1,0:T(8,128)S(1)}, u32[]{:S(2)}, u32[]{:S(2)}) collective-permute-start(f32[1,128,128]{2,1,0:T(8,128)S(1)} %slice.494), channel_id=1, source_target_pairs={{0,16},{16,0},{1,17},{17,1},{2,18},{18,2},{3,19},{19,3},{4,20},{20... | collective-permute-start | bytes 196616 | tf_op jit(solution)/shard_map/ppermute | solution.py:19
  432.7 9.8 %collective-permute-start.41 = (f32[1,128,128]{2,1,0:T(8,128)S(1)}, f32[1,128,128]{2,1,0:T(8,128)S(1)}, u32[]{:S(2)}, u32[]{:S(2)}) collective-permute-start(f32[1,128,128]{2,1,0:T(8,128)S(1)} %get-tuple-element.22), channel_id=1, source_target_pairs={{1,0},{2,1},{3,2},{0,3},{5,4},{6,5},{7,6},{4,7},{9,8},{10,9},{11,1... | collective-permute-start | bytes 196616 | tf_op jit(solution)/shard_map/ppermute | solution.py:20
  432.8 9.7 %collective-permute-start.40 = (f32[1,128,128]{2,1,0:T(8,128)S(1)}, f32[1,128,128]{2,1,0:T(8,128)S(1)}, u32[]{:S(2)}, u32[]{:S(2)}) collective-permute-start(f32[1,128,128]{2,1,0:T(8,128)S(1)} %get-tuple-element.24), channel_id=1, source_target_pairs={{0,1},{1,2},{2,3},{3,0},{4,5},{5,6},{6,7},{7,4},{8,9},{9,10},{10,1... | collective-permute-start | bytes 196616 | tf_op jit(solution)/shard_map/ppermute | solution.py:19
  433.3 9.1 %collective-permute-start.38 = (f32[1,128,128]{2,1,0:T(8,128)S(1)}, f32[1,128,128]{2,1,0:T(8,128)S(1)}, u32[]{:S(2)}, u32[]{:S(2)}) collective-permute-start(f32[1,128,128]{2,1,0:T(8,128)S(1)} %get-tuple-element.25), channel_id=1, source_target_pairs={{0,4},{4,8},{8,12},{12,0},{1,5},{5,9},{9,13},{13,1},{2,6},{6,10},{... | collective-permute-start | bytes 196616 | tf_op jit(solution)/shard_map/ppermute | solution.py:19
  433.3 9.1 %collective-permute-start.39 = (f32[1,128,128]{2,1,0:T(8,128)S(1)}, f32[1,128,128]{2,1,0:T(8,128)S(1)}, u32[]{:S(2)}, u32[]{:S(2)}) collective-permute-start(f32[1,128,128]{2,1,0:T(8,128)S(1)} %get-tuple-element.26), channel_id=1, source_target_pairs={{4,0},{8,4},{12,8},{0,12},{5,1},{9,5},{13,9},{1,13},{6,2},{10,6},{... | collective-permute-start | bytes 196616 | tf_op jit(solution)/shard_map/ppermute | solution.py:20
  543.0 7.1 %collective-permute-start.47 = (f32[1,128,128]{2,1,0:T(8,128)S(1)}, f32[1,128,128]{2,1,0:T(8,128)S(1)}, u32[]{:S(2)}, u32[]{:S(2)}) collective-permute-start(f32[1,128,128]{2,1,0:T(8,128)S(1)} %get-tuple-element.16), channel_id=1, source_target_pairs={{1,0},{2,1},{3,2},{0,3},{5,4},{6,5},{7,6},{4,7},{9,8},{10,9},{11,1... | collective-permute-start | bytes 196616 | tf_op jit(solution)/shard_map/ppermute | solution.py:20
  543.1 7.0 %collective-permute-start.46 = (f32[1,128,128]{2,1,0:T(8,128)S(1)}, f32[1,128,128]{2,1,0:T(8,128)S(1)}, u32[]{:S(2)}, u32[]{:S(2)}) collective-permute-start(f32[1,128,128]{2,1,0:T(8,128)S(1)} %get-tuple-element.18), channel_id=1, source_target_pairs={{0,1},{1,2},{2,3},{3,0},{4,5},{5,6},{6,7},{7,4},{8,9},{9,10},{10,1... | collective-permute-start | bytes 196616 | tf_op jit(solution)/shard_map/ppermute | solution.py:19
  591.7 8.7 %collective-permute-start.48 = (f32[1,128,128]{2,1,0:T(8,128)S(1)}, f32[1,128,128]{2,1,0:T(8,128)S(1)}, u32[]{:S(2)}, u32[]{:S(2)}) collective-permute-start(f32[1,128,128]{2,1,0:T(8,128)S(1)} %slice.509), channel_id=1, source_target_pairs={{0,16},{16,0},{1,17},{17,1},{2,18},{18,2},{3,19},{19,3},{4,20},{20... | collective-permute-start | bytes 196616 | tf_op jit(solution)/shard_map/ppermute | solution.py:19
  600.4 9.8 %collective-permute-start.53 = (f32[1,128,128]{2,1,0:T(8,128)S(1)}, f32[1,128,128]{2,1,0:T(8,128)S(1)}, u32[]{:S(2)}, u32[]{:S(2)}) collective-permute-start(f32[1,128,128]{2,1,0:T(8,128)S(1)} %get-tuple-element.10), channel_id=1, source_target_pairs={{1,0},{2,1},{3,2},{0,3},{5,4},{6,5},{7,6},{4,7},{9,8},{10,9},{11,1... | collective-permute-start | bytes 196616 | tf_op jit(solution)/shard_map/ppermute | solution.py:20
  600.5 9.7 %collective-permute-start.52 = (f32[1,128,128]{2,1,0:T(8,128)S(1)}, f32[1,128,128]{2,1,0:T(8,128)S(1)}, u32[]{:S(2)}, u32[]{:S(2)}) collective-permute-start(f32[1,128,128]{2,1,0:T(8,128)S(1)} %get-tuple-element.12), channel_id=1, source_target_pairs={{0,1},{1,2},{2,3},{3,0},{4,5},{5,6},{6,7},{7,4},{8,9},{9,10},{10,1... | collective-permute-start | bytes 196616 | tf_op jit(solution)/shard_map/ppermute | solution.py:19
  601.0 9.1 %collective-permute-start.50 = (f32[1,128,128]{2,1,0:T(8,128)S(1)}, f32[1,128,128]{2,1,0:T(8,128)S(1)}, u32[]{:S(2)}, u32[]{:S(2)}) collective-permute-start(f32[1,128,128]{2,1,0:T(8,128)S(1)} %get-tuple-element.13), channel_id=1, source_target_pairs={{0,4},{4,8},{8,12},{12,0},{1,5},{5,9},{9,13},{13,1},{2,6},{6,10},{... | collective-permute-start | bytes 196616 | tf_op jit(solution)/shard_map/ppermute | solution.py:19
  601.0 9.1 %collective-permute-start.51 = (f32[1,128,128]{2,1,0:T(8,128)S(1)}, f32[1,128,128]{2,1,0:T(8,128)S(1)}, u32[]{:S(2)}, u32[]{:S(2)}) collective-permute-start(f32[1,128,128]{2,1,0:T(8,128)S(1)} %get-tuple-element.14), channel_id=1, source_target_pairs={{4,0},{8,4},{12,8},{0,12},{5,1},{9,5},{13,9},{1,13},{6,2},{10,6},{... | collective-permute-start | bytes 196616 | tf_op jit(solution)/shard_map/ppermute | solution.py:20
  (118 other events, 1049.8 us)
where the time goes:
time: 668 us; the launch traced here: 666 us
  blocking collectives  442 us (66%)
  other arithmetic  60.4 us (9%)
  starting transfers between devices  49.7 us (7%)
  waiting for transfers between devices  45.8 us (7%)
  matrix products  34.5 us (5%)
  local copies, waits for them, and re-layouts  29.8 us (4%)
    all_gather x5, blocking collectives, coarse_solve(): lax.all_gather(loads, ('gx', 'gy', 'gz'), axis=0, tiled=True)  192 us
    psum x3, blocking collectives, per_device(): lax.psum(jnp.stack([plus_inner(direction, image_now), plus_inner(directio...  127 us
    psum x3, blocking collectives, per_device(): totals = lax.psum(local_rows, ('gx', 'gy', 'gz'))  122 us
    unnamed x76, other arithmetic  32.8 us
    ppermute x27, starting transfers between devices, extended(): after = lax.ppermute(initial, axis, down)  29.9 us
    ppermute x27, waiting for transfers between devices, extended(): after = lax.ppermute(initial, axis, down)  28.2 us
    ppermute x27, starting transfers between devices, extended(): before = lax.ppermute(last, axis, up)  19.8 us
    ppermute x27, waiting for transfers between devices, extended(): before = lax.ppermute(last, axis, up)  17.5 us
  transfers between devices with their start and end apart: 54, of which 15 were waited for; matrix products, arithmetic and copies ran while one was open for 9% of the time, Pallas kernels for 0%

commit v1 on v0

--- a/solution.py
+++ b/solution.py
@@ -100,7 +100,7 @@
         if images:
             own_rows = jnp.stack([plus_inner(images[index], resid) for index in range(len(images))])
             local_rows = jnp.concatenate([local_rows, own_rows], axis=0)
-        totals = lax.psum(local_rows, ("gx", "gy", "gz"))
+        totals = lax.psum(lax.psum(local_rows, "gx"), ("gy", "gz"))
         beta = totals[:STORED] / stored_curv[:, None]
         direction = resid - jnp.einsum("isf,ir->sfr", dirs_store, beta, precision=precise)
         for index in range(len(directions)):

time: 668 us -> 737 us (1.10)
  blocking collectives: 442 us -> 489 us
  starting transfers between devices: 49.7 us -> 82.2 us
  waiting for transfers between devices: 45.8 us -> 31.7 us
    psum x3 -> x6, blocking collectives: 122 us -> 172 us  [per_device(): totals = lax.psum(lax.psum(local_rows, 'gx'), ('gy', 'gz'))]
    ppermute x27, starting transfers between devices: 29.9 us -> 60.9 us  [extended(): after = lax.ppermute(initial, axis, down)]
    ppermute x27, waiting for transfers between devices: 17.5 us -> 9.65 us  [extended(): before = lax.ppermute(last, axis, up)]
  transfers between devices with their start and end apart: 54 -> 54, of which waited for: 15 -> 14; matrix products, arithmetic and copies ran while one was open for 9% -> 8% of each run, Pallas kernels for 0% -> 0%
where the time goes in v1:
time: 737 us; the launch traced here: 735 us
  blocking collectives  489 us (66%)
  starting transfers between devices  82.2 us (11%)
  other arithmetic  64.4 us (9%)
  matrix products  34.5 us (5%)
  waiting for transfers between devices  31.7 us (4%)
  local copies, waits for them, and re-layouts  29.9 us (4%)
    all_gather x5, blocking collectives, coarse_solve(): lax.all_gather(loads, ('gx', 'gy', 'gz'), axis=0, tiled=True)  187 us
    psum x6, blocking collectives, per_device(): totals = lax.psum(lax.psum(local_rows, 'gx'), ('gy', 'gz'))  172 us
    psum x3, blocking collectives, per_device(): lax.psum(jnp.stack([plus_inner(direction, image_now), plus_inner(directio...  129 us
    ppermute x27, starting transfers between devices, extended(): after = lax.ppermute(initial, axis, down)  60.9 us
    unnamed x76, other arithmetic  36.1 us
    ppermute x27, waiting for transfers between devices, extended(): after = lax.ppermute(initial, axis, down)  22 us
    ppermute x27, starting transfers between devices, extended(): before = lax.ppermute(last, axis, up)  21.2 us
    dot_general x4, matrix products, operate(): return jnp.dot(flex_face, flat, precision=precise).reshape(layout)  14.8 us
  transfers between devices with their start and end apart: 54, of which 14 were waited for; matrix products, arithmetic and copies ran while one was open for 8% of the time, Pallas kernels for 0%

profile of v1, /device:TPU:10, one launch (start us, length us, event | category | flops | bytes accessed | tf_op | source)
XLA Modules:
  0.0 734.7 jit_solution(1976140282468337180)
XLA Ops:
  1.5 37.6 %all-gather = f32[1,1,1,192,128]{4,2,1,0,3:T(1,128)S(1)} all-gather(f32[1,1,1,6,128]{4,2,1,0,3:T(1,128)} %bitcast.275), channel_id=2, replica_groups=mesh['gx'=2,'gy'=4,'gz'=4] {'gx','gy','gz'}, dimensions={3}, use_global_device_ids=true | all-gather | bytes 101376 | tf_op jit(solution)/shard_map/all_gather | solution.py:51
  43.9 3.4 scatter_custom_fusion
  47.3 3.5 gather_fusion
  57.1 5.7 gather_fusion.1
  71.2 4.2 collective-permute-start.3
  78.8 3.7 fusion.4
  87.5 4.6 collective-permute-start.8
  99.1 37.6 %all-gather.1 = f32[32,6,128]{2,1,0:T(8,128)S(1)} all-gather(f32[1,6,128]{2,1,0:T(8,128)S(1)} %convolution_bitcast_fusion.14), channel_id=1, replica_groups=mesh['gx'=2,'gy'=4,'gz'=4] {'gx','gy','gz'}, dimensions={0}, use_global_device_ids=true | all-gather | bytes 101376 | tf_op jit(solution)/shard_map/all_gather | solution.py:51
  142.7 4.2 collective-permute-start.15
  153.0 8.1 %psum.63 = f32[40,128]{1,0:T(8,128)S(1)} all-reduce(f32[40,128]{1,0:T(8,128)S(1)} %convolution_bitcast_fusion.5), channel_id=1, replica_groups=mesh['gx'=2,'gy'=4,'gz'=4] {'gx'}, use_global_device_ids=true, to_apply=%region_1.2 | all-reduce | flops 5120 | bytes 40960 | tf_op jit(solution)/shard_map/psum | solution.py:103
  161.1 53.1 %psum.64 = f32[40,128]{1,0:T(8,128)} all-reduce(f32[40,128]{1,0:T(8,128)S(1)} %psum.63), channel_id=1, replica_groups=mesh['gx'=2,'gy'=4,'gz'=4] {'gy','gz'}, use_global_device_ids=true, to_apply=%region_2.3 | all-reduce | flops 5120 | bytes 40960 | tf_op jit(solution)/shard_map/psum | solution.py:103
  216.0 3.7 convolution_multiply_fusion.2
  225.0 8.4 %collective-permute-start.21 = (f32[1,128,128]{2,1,0:T(8,128)S(1)}, f32[1,128,128]{2,1,0:T(8,128)S(1)}, u32[]{:S(2)}, u32[]{:S(2)}) collective-permute-start(f32[1,128,128]{2,1,0:T(8,128)S(1)} %get-tuple-element.44), channel_id=1, source_target_pairs={{4,0},{8,4},{12,8},{0,12},{5,1},{9,5},{13,9},{1,13},{6,2},{10,6},{... | collective-permute-start | bytes 196616 | tf_op jit(solution)/shard_map/ppermute | solution.py:20
  238.5 39.0 %all-gather.2 = f32[32,6,128]{2,1,0:T(8,128)} all-gather(f32[1,6,128]{2,1,0:T(8,128)S(1)} %convolution_bitcast_fusion.13), channel_id=1, replica_groups=mesh['gx'=2,'gy'=4,'gz'=4] {'gx','gy','gz'}, dimensions={0}, use_global_device_ids=true | all-gather | bytes 101376 | tf_op jit(solution)/shard_map/all_gather | solution.py:51
  292.5 4.2 collective-permute-start.27
  303.1 43.1 %psum.65 = f32[2,128]{1,0:T(2,128)S(1)} all-reduce(f32[2,128]{1,0:T(2,128)S(1)} %pad_maximum_fusion.2), channel_id=1, replica_groups=mesh['gx'=2,'gy'=4,'gz'=4] {'gx','gy','gz'}, use_global_device_ids=true, to_apply=%region_5.6 | all-reduce | flops 256 | bytes 2048 | tf_op jit(solution)/shard_map/psum | solution.py:109
  350.0 6.9 psum.66
  356.8 48.8 %psum.67 = f32[41,128]{1,0:T(8,128)S(1)} all-reduce(f32[41,128]{1,0:T(8,128)S(1)} %psum.66), channel_id=1, replica_groups=mesh['gx'=2,'gy'=4,'gz'=4] {'gy','gz'}, use_global_device_ids=true, to_apply=%region_8.9 | all-reduce | flops 5248 | bytes 41984 | tf_op jit(solution)/shard_map/psum | solution.py:103
  408.9 3.7 convolution_multiply_fusion.1
  417.5 8.5 %collective-permute-start.33 = (f32[1,128,128]{2,1,0:T(8,128)S(1)}, f32[1,128,128]{2,1,0:T(8,128)S(1)}, u32[]{:S(2)}, u32[]{:S(2)}) collective-permute-start(f32[1,128,128]{2,1,0:T(8,128)S(1)} %get-tuple-element.32), channel_id=1, source_target_pairs={{4,0},{8,4},{12,8},{0,12},{5,1},{9,5},{13,9},{1,13},{6,2},{10,6},{... | collective-permute-start | bytes 196616 | tf_op jit(solution)/shard_map/ppermute | solution.py:20
  431.2 36.4 %all-gather.3 = f32[32,6,128]{2,1,0:T(8,128)S(1)} all-gather(f32[1,6,128]{2,1,0:T(8,128)S(1)} %convolution_bitcast_fusion.12), channel_id=1, replica_groups=mesh['gx'=2,'gy'=4,'gz'=4] {'gx','gy','gz'}, dimensions={0}, use_global_device_ids=true | all-gather | bytes 101376 | tf_op jit(solution)/shard_map/all_gather | solution.py:51
  480.5 4.2 collective-permute-start.39
  485.6 3.3 collective-permute-done.37
  491.7 43.3 %psum.68 = f32[2,128]{1,0:T(2,128)} all-reduce(f32[2,128]{1,0:T(2,128)} %pad_maximum_fusion.3), channel_id=1, replica_groups=mesh['gx'=2,'gy'=4,'gz'=4] {'gx','gy','gz'}, use_global_device_ids=true, to_apply=%region_11.12 | all-reduce | flops 256 | bytes 2048 | tf_op jit(solution)/shard_map/psum | solution.py:109
  539.2 6.8 psum.69
  546.0 48.7 %psum.70 = f32[42,128]{1,0:T(8,128)S(1)} all-reduce(f32[42,128]{1,0:T(8,128)S(1)} %psum.69), channel_id=1, replica_groups=mesh['gx'=2,'gy'=4,'gz'=4] {'gy','gz'}, use_global_device_ids=true, to_apply=%region_15.16 | all-reduce | flops 5376 | bytes 43008 | tf_op jit(solution)/shard_map/psum | solution.py:103
  598.3 3.7 convolution_multiply_fusion
  606.9 8.4 %collective-permute-start.45 = (f32[1,128,128]{2,1,0:T(8,128)S(1)}, f32[1,128,128]{2,1,0:T(8,128)S(1)}, u32[]{:S(2)}, u32[]{:S(2)}) collective-permute-start(f32[1,128,128]{2,1,0:T(8,128)S(1)} %get-tuple-element.20), channel_id=1, source_target_pairs={{4,0},{8,4},{12,8},{0,12},{5,1},{9,5},{13,9},{1,13},{6,2},{10,6},{... | collective-permute-start | bytes 196616 | tf_op jit(solution)/shard_map/ppermute | solution.py:20
  620.6 36.5 %all-gather.4 = f32[32,6,128]{2,1,0:T(8,128)S(1)} all-gather(f32[1,6,128]{2,1,0:T(8,128)S(1)} %convolution_bitcast_fusion.11), channel_id=1, replica_groups=mesh['gx'=2,'gy'=4,'gz'=4] {'gx','gy','gz'}, dimensions={0}, use_global_device_ids=true | all-gather | bytes 101376 | tf_op jit(solution)/shard_map/all_gather | solution.py:51
  670.1 4.2 collective-permute-start.51
  675.2 3.3 collective-permute-done.49
  680.1 43.1 %psum.71 = f32[2,128]{1,0:T(2,128)S(1)} all-reduce(f32[2,128]{1,0:T(2,128)S(1)} %pad_maximum_fusion.4), channel_id=1, replica_groups=mesh['gx'=2,'gy'=4,'gz'=4] {'gx','gy','gz'}, use_global_device_ids=true, to_apply=%region_18.19 | all-reduce | flops 256 | bytes 2048 | tf_op jit(solution)/shard_map/psum | solution.py:109
  (453 shorter events, 157.9 us)
Async XLA Ops:
  41.6 21.3 %collective-permute-start = (f32[1,128,128]{2,1,0:T(8,128)S(1)}, f32[1,128,128]{2,1,0:T(8,128)}, u32[]{:S(2)}, u32[]{:S(2)}) collective-permute-start(f32[1,128,128]{2,1,0:T(8,128)S(1)} %slice.456), channel_id=1, source_target_pairs={{0,16},{16,0},{1,17},{17,1},{2,18},{18,2},{3,19},{19,3},{4,20},{20... | collective-permute-start | bytes 196616 | tf_op jit(solution)/shard_map/ppermute | solution.py:19
  63.7 11.6 %collective-permute-start.1 = (f32[1,128,128]{2,1,0:T(8,128)S(1)}, f32[1,128,128]{2,1,0:T(8,128)}, u32[]{:S(2)}, u32[]{:S(2)}) collective-permute-start(f32[1,128,128]{2,1,0:T(8,128)S(1)} %get-tuple-element.63), channel_id=1, source_target_pairs={{16,0},{0,16},{17,1},{1,17},{18,2},{2,18},{19,3},{3,19},{20,4},{4,... | collective-permute-start | bytes 196616 | tf_op jit(solution)/shard_map/ppermute | solution.py:20
  86.9 11.1 %collective-permute-start.11 = (f32[1,128,128]{2,1,0:T(8,128)S(1)}, f32[1,128,128]{2,1,0:T(8,128)S(1)}, u32[]{:S(2)}, u32[]{:S(2)}) collective-permute-start(f32[1,128,128]{2,1,0:T(8,128)S(1)} %get-tuple-element.52), channel_id=1, source_target_pairs={{1,0},{2,1},{3,2},{0,3},{5,4},{6,5},{7,6},{4,7},{9,8},{10,9},{11,1... | collective-permute-start | bytes 196616 | tf_op jit(solution)/shard_map/ppermute | solution.py:20
  87.0 11.0 %collective-permute-start.10 = (f32[1,128,128]{2,1,0:T(8,128)S(1)}, f32[1,128,128]{2,1,0:T(8,128)S(1)}, u32[]{:S(2)}, u32[]{:S(2)}) collective-permute-start(f32[1,128,128]{2,1,0:T(8,128)S(1)} %get-tuple-element.54), channel_id=1, source_target_pairs={{0,1},{1,2},{2,3},{3,0},{4,5},{5,6},{6,7},{7,4},{8,9},{9,10},{10,1... | collective-permute-start | bytes 196616 | tf_op jit(solution)/shard_map/ppermute | solution.py:19
  87.5 8.9 %collective-permute-start.8 = (f32[1,128,128]{2,1,0:T(8,128)S(1)}, f32[1,128,128]{2,1,0:T(8,128)S(1)}, u32[]{:S(2)}, u32[]{:S(2)}) collective-permute-start(f32[1,128,128]{2,1,0:T(8,128)S(1)} %get-tuple-element.55), channel_id=1, source_target_pairs={{0,4},{4,8},{8,12},{12,0},{1,5},{5,9},{9,13},{13,1},{2,6},{6,10},{... | collective-permute-start | bytes 196616 | tf_op jit(solution)/shard_map/ppermute | solution.py:19
  142.2 9.3 %collective-permute-start.17 = (f32[1,128,128]{2,1,0:T(8,128)S(1)}, f32[1,128,128]{2,1,0:T(8,128)S(1)}, u32[]{:S(2)}, u32[]{:S(2)}) collective-permute-start(f32[1,128,128]{2,1,0:T(8,128)S(1)} %get-tuple-element.46), channel_id=1, source_target_pairs={{1,0},{2,1},{3,2},{0,3},{5,4},{6,5},{7,6},{4,7},{9,8},{10,9},{11,1... | collective-permute-start | bytes 196616 | tf_op jit(solution)/shard_map/ppermute | solution.py:20
  142.2 9.2 %collective-permute-start.16 = (f32[1,128,128]{2,1,0:T(8,128)S(1)}, f32[1,128,128]{2,1,0:T(8,128)S(1)}, u32[]{:S(2)}, u32[]{:S(2)}) collective-permute-start(f32[1,128,128]{2,1,0:T(8,128)S(1)} %get-tuple-element.48), channel_id=1, source_target_pairs={{0,1},{1,2},{2,3},{3,0},{4,5},{5,6},{6,7},{7,4},{8,9},{9,10},{10,1... | collective-permute-start | bytes 196616 | tf_op jit(solution)/shard_map/ppermute | solution.py:19
  142.7 8.6 %collective-permute-start.14 = (f32[1,128,128]{2,1,0:T(8,128)S(1)}, f32[1,128,128]{2,1,0:T(8,128)S(1)}, u32[]{:S(2)}, u32[]{:S(2)}) collective-permute-start(f32[1,128,128]{2,1,0:T(8,128)S(1)} %get-tuple-element.49), channel_id=1, source_target_pairs={{0,4},{4,8},{8,12},{12,0},{1,5},{5,9},{9,13},{13,1},{2,6},{6,10},{... | collective-permute-start | bytes 196616 | tf_op jit(solution)/shard_map/ppermute | solution.py:19
  142.7 8.7 %collective-permute-start.15 = (f32[1,128,128]{2,1,0:T(8,128)S(1)}, f32[1,128,128]{2,1,0:T(8,128)S(1)}, u32[]{:S(2)}, u32[]{:S(2)}) collective-permute-start(f32[1,128,128]{2,1,0:T(8,128)S(1)} %get-tuple-element.50), channel_id=1, source_target_pairs={{4,0},{8,4},{12,8},{0,12},{5,1},{9,5},{13,9},{1,13},{6,2},{10,6},{... | collective-permute-start | bytes 196616 | tf_op jit(solution)/shard_map/ppermute | solution.py:20
  224.5 13.4 %collective-permute-start.23 = (f32[1,128,128]{2,1,0:T(8,128)S(1)}, f32[1,128,128]{2,1,0:T(8,128)S(1)}, u32[]{:S(2)}, u32[]{:S(2)}) collective-permute-start(f32[1,128,128]{2,1,0:T(8,128)S(1)} %get-tuple-element.40), channel_id=1, source_target_pairs={{1,0},{2,1},{3,2},{0,3},{5,4},{6,5},{7,6},{4,7},{9,8},{10,9},{11,1... | collective-permute-start | bytes 196616 | tf_op jit(solution)/shard_map/ppermute | solution.py:20
  224.5 13.3 %collective-permute-start.22 = (f32[1,128,128]{2,1,0:T(8,128)S(1)}, f32[1,128,128]{2,1,0:T(8,128)S(1)}, u32[]{:S(2)}, u32[]{:S(2)}) collective-permute-start(f32[1,128,128]{2,1,0:T(8,128)S(1)} %get-tuple-element.42), channel_id=1, source_target_pairs={{0,1},{1,2},{2,3},{3,0},{4,5},{5,6},{6,7},{7,4},{8,9},{9,10},{10,1... | collective-permute-start | bytes 196616 | tf_op jit(solution)/shard_map/ppermute | solution.py:19
  225.0 12.7 %collective-permute-start.20 = (f32[1,128,128]{2,1,0:T(8,128)S(1)}, f32[1,128,128]{2,1,0:T(8,128)S(1)}, u32[]{:S(2)}, u32[]{:S(2)}) collective-permute-start(f32[1,128,128]{2,1,0:T(8,128)S(1)} %get-tuple-element.43), channel_id=1, source_target_pairs={{0,4},{4,8},{8,12},{12,0},{1,5},{5,9},{9,13},{13,1},{2,6},{6,10},{... | collective-permute-start | bytes 196616 | tf_op jit(solution)/shard_map/ppermute | solution.py:19
  225.0 12.8 %collective-permute-start.21 = (f32[1,128,128]{2,1,0:T(8,128)S(1)}, f32[1,128,128]{2,1,0:T(8,128)S(1)}, u32[]{:S(2)}, u32[]{:S(2)}) collective-permute-start(f32[1,128,128]{2,1,0:T(8,128)S(1)} %get-tuple-element.44), channel_id=1, source_target_pairs={{4,0},{8,4},{12,8},{0,12},{5,1},{9,5},{13,9},{1,13},{6,2},{10,6},{... | collective-permute-start | bytes 196616 | tf_op jit(solution)/shard_map/ppermute | solution.py:20
  281.7 9.0 %collective-permute-start.24 = (f32[1,128,128]{2,1,0:T(8,128)S(1)}, f32[1,128,128]{2,1,0:T(8,128)S(1)}, u32[]{:S(2)}, u32[]{:S(2)}) collective-permute-start(f32[1,128,128]{2,1,0:T(8,128)S(1)} %slice.480), channel_id=1, source_target_pairs={{0,16},{16,0},{1,17},{17,1},{2,18},{18,2},{3,19},{19,3},{4,20},{20... | collective-permute-start | bytes 196616 | tf_op jit(solution)/shard_map/ppermute | solution.py:19
  290.7 10.3 %collective-permute-start.29 = (f32[1,128,128]{2,1,0:T(8,128)S(1)}, f32[1,128,128]{2,1,0:T(8,128)S(1)}, u32[]{:S(2)}, u32[]{:S(2)}) collective-permute-start(f32[1,128,128]{2,1,0:T(8,128)S(1)} %get-tuple-element.34), channel_id=1, source_target_pairs={{1,0},{2,1},{3,2},{0,3},{5,4},{6,5},{7,6},{4,7},{9,8},{10,9},{11,1... | collective-permute-start | bytes 196616 | tf_op jit(solution)/shard_map/ppermute | solution.py:20
  292.5 8.5 %collective-permute-start.28 = (f32[1,128,128]{2,1,0:T(8,128)S(1)}, f32[1,128,128]{2,1,0:T(8,128)S(1)}, u32[]{:S(2)}, u32[]{:S(2)}) collective-permute-start(f32[1,128,128]{2,1,0:T(8,128)S(1)} %get-tuple-element.36), channel_id=1, source_target_pairs={{0,1},{1,2},{2,3},{3,0},{4,5},{5,6},{6,7},{7,4},{8,9},{9,10},{10,1... | collective-permute-start | bytes 196616 | tf_op jit(solution)/shard_map/ppermute | solution.py:19
  292.5 8.5 %collective-permute-start.27 = (f32[1,128,128]{2,1,0:T(8,128)S(1)}, f32[1,128,128]{2,1,0:T(8,128)S(1)}, u32[]{:S(2)}, u32[]{:S(2)}) collective-permute-start(f32[1,128,128]{2,1,0:T(8,128)S(1)} %get-tuple-element.38), channel_id=1, source_target_pairs={{4,0},{8,4},{12,8},{0,12},{5,1},{9,5},{13,9},{1,13},{6,2},{10,6},{... | collective-permute-start | bytes 196616 | tf_op jit(solution)/shard_map/ppermute | solution.py:20
  417.0 13.4 %collective-permute-start.35 = (f32[1,128,128]{2,1,0:T(8,128)S(1)}, f32[1,128,128]{2,1,0:T(8,128)S(1)}, u32[]{:S(2)}, u32[]{:S(2)}) collective-permute-start(f32[1,128,128]{2,1,0:T(8,128)S(1)} %get-tuple-element.28), channel_id=1, source_target_pairs={{1,0},{2,1},{3,2},{0,3},{5,4},{6,5},{7,6},{4,7},{9,8},{10,9},{11,1... | collective-permute-start | bytes 196616 | tf_op jit(solution)/shard_map/ppermute | solution.py:20
  417.0 13.3 %collective-permute-start.34 = (f32[1,128,128]{2,1,0:T(8,128)S(1)}, f32[1,128,128]{2,1,0:T(8,128)S(1)}, u32[]{:S(2)}, u32[]{:S(2)}) collective-permute-start(f32[1,128,128]{2,1,0:T(8,128)S(1)} %get-tuple-element.30), channel_id=1, source_target_pairs={{0,1},{1,2},{2,3},{3,0},{4,5},{5,6},{6,7},{7,4},{8,9},{9,10},{10,1... | collective-permute-start | bytes 196616 | tf_op jit(solution)/shard_map/ppermute | solution.py:19
  417.5 12.7 %collective-permute-start.32 = (f32[1,128,128]{2,1,0:T(8,128)S(1)}, f32[1,128,128]{2,1,0:T(8,128)S(1)}, u32[]{:S(2)}, u32[]{:S(2)}) collective-permute-start(f32[1,128,128]{2,1,0:T(8,128)S(1)} %get-tuple-element.31), channel_id=1, source_target_pairs={{0,4},{4,8},{8,12},{12,0},{1,5},{5,9},{9,13},{13,1},{2,6},{6,10},{... | collective-permute-start | bytes 196616 | tf_op jit(solution)/shard_map/ppermute | solution.py:19
  417.5 12.8 %collective-permute-start.33 = (f32[1,128,128]{2,1,0:T(8,128)S(1)}, f32[1,128,128]{2,1,0:T(8,128)S(1)}, u32[]{:S(2)}, u32[]{:S(2)}) collective-permute-start(f32[1,128,128]{2,1,0:T(8,128)S(1)} %get-tuple-element.32), channel_id=1, source_target_pairs={{4,0},{8,4},{12,8},{0,12},{5,1},{9,5},{13,9},{1,13},{6,2},{10,6},{... | collective-permute-start | bytes 196616 | tf_op jit(solution)/shard_map/ppermute | solution.py:20
  469.4 9.4 %collective-permute-start.36 = (f32[1,128,128]{2,1,0:T(8,128)S(1)}, f32[1,128,128]{2,1,0:T(8,128)S(1)}, u32[]{:S(2)}, u32[]{:S(2)}) collective-permute-start(f32[1,128,128]{2,1,0:T(8,128)S(1)} %slice.494), channel_id=1, source_target_pairs={{0,16},{16,0},{1,17},{17,1},{2,18},{18,2},{3,19},{19,3},{4,20},{20... | collective-permute-start | bytes 196616 | tf_op jit(solution)/shard_map/ppermute | solution.py:19
  478.9 10.2 %collective-permute-start.41 = (f32[1,128,128]{2,1,0:T(8,128)S(1)}, f32[1,128,128]{2,1,0:T(8,128)S(1)}, u32[]{:S(2)}, u32[]{:S(2)}) collective-permute-start(f32[1,128,128]{2,1,0:T(8,128)S(1)} %get-tuple-element.22), channel_id=1, source_target_pairs={{1,0},{2,1},{3,2},{0,3},{5,4},{6,5},{7,6},{4,7},{9,8},{10,9},{11,1... | collective-permute-start | bytes 196616 | tf_op jit(solution)/shard_map/ppermute | solution.py:20
  480.5 8.5 %collective-permute-start.40 = (f32[1,128,128]{2,1,0:T(8,128)S(1)}, f32[1,128,128]{2,1,0:T(8,128)S(1)}, u32[]{:S(2)}, u32[]{:S(2)}) collective-permute-start(f32[1,128,128]{2,1,0:T(8,128)S(1)} %get-tuple-element.24), channel_id=1, source_target_pairs={{0,1},{1,2},{2,3},{3,0},{4,5},{5,6},{6,7},{7,4},{8,9},{9,10},{10,1... | collective-permute-start | bytes 196616 | tf_op jit(solution)/shard_map/ppermute | solution.py:19
  480.5 8.5 %collective-permute-start.39 = (f32[1,128,128]{2,1,0:T(8,128)S(1)}, f32[1,128,128]{2,1,0:T(8,128)S(1)}, u32[]{:S(2)}, u32[]{:S(2)}) collective-permute-start(f32[1,128,128]{2,1,0:T(8,128)S(1)} %get-tuple-element.26), channel_id=1, source_target_pairs={{4,0},{8,4},{12,8},{0,12},{5,1},{9,5},{13,9},{1,13},{6,2},{10,6},{... | collective-permute-start | bytes 196616 | tf_op jit(solution)/shard_map/ppermute | solution.py:20
  606.4 13.4 %collective-permute-start.47 = (f32[1,128,128]{2,1,0:T(8,128)S(1)}, f32[1,128,128]{2,1,0:T(8,128)S(1)}, u32[]{:S(2)}, u32[]{:S(2)}) collective-permute-start(f32[1,128,128]{2,1,0:T(8,128)S(1)} %get-tuple-element.16), channel_id=1, source_target_pairs={{1,0},{2,1},{3,2},{0,3},{5,4},{6,5},{7,6},{4,7},{9,8},{10,9},{11,1... | collective-permute-start | bytes 196616 | tf_op jit(solution)/shard_map/ppermute | solution.py:20
  606.4 13.3 %collective-permute-start.46 = (f32[1,128,128]{2,1,0:T(8,128)S(1)}, f32[1,128,128]{2,1,0:T(8,128)S(1)}, u32[]{:S(2)}, u32[]{:S(2)}) collective-permute-start(f32[1,128,128]{2,1,0:T(8,128)S(1)} %get-tuple-element.18), channel_id=1, source_target_pairs={{0,1},{1,2},{2,3},{3,0},{4,5},{5,6},{6,7},{7,4},{8,9},{9,10},{10,1... | collective-permute-start | bytes 196616 | tf_op jit(solution)/shard_map/ppermute | solution.py:19
  606.9 12.7 %collective-permute-start.44 = (f32[1,128,128]{2,1,0:T(8,128)S(1)}, f32[1,128,128]{2,1,0:T(8,128)S(1)}, u32[]{:S(2)}, u32[]{:S(2)}) collective-permute-start(f32[1,128,128]{2,1,0:T(8,128)S(1)} %get-tuple-element.19), channel_id=1, source_target_pairs={{0,4},{4,8},{8,12},{12,0},{1,5},{5,9},{9,13},{13,1},{2,6},{6,10},{... | collective-permute-start | bytes 196616 | tf_op jit(solution)/shard_map/ppermute | solution.py:19
  606.9 12.8 %collective-permute-start.45 = (f32[1,128,128]{2,1,0:T(8,128)S(1)}, f32[1,128,128]{2,1,0:T(8,128)S(1)}, u32[]{:S(2)}, u32[]{:S(2)}) collective-permute-start(f32[1,128,128]{2,1,0:T(8,128)S(1)} %get-tuple-element.20), channel_id=1, source_target_pairs={{4,0},{8,4},{12,8},{0,12},{5,1},{9,5},{13,9},{1,13},{6,2},{10,6},{... | collective-permute-start | bytes 196616 | tf_op jit(solution)/shard_map/ppermute | solution.py:20
  659.0 9.4 %collective-permute-start.48 = (f32[1,128,128]{2,1,0:T(8,128)S(1)}, f32[1,128,128]{2,1,0:T(8,128)S(1)}, u32[]{:S(2)}, u32[]{:S(2)}) collective-permute-start(f32[1,128,128]{2,1,0:T(8,128)S(1)} %slice.509), channel_id=1, source_target_pairs={{0,16},{16,0},{1,17},{17,1},{2,18},{18,2},{3,19},{19,3},{4,20},{20... | collective-permute-start | bytes 196616 | tf_op jit(solution)/shard_map/ppermute | solution.py:19
  668.4 10.3 %collective-permute-start.53 = (f32[1,128,128]{2,1,0:T(8,128)S(1)}, f32[1,128,128]{2,1,0:T(8,128)S(1)}, u32[]{:S(2)}, u32[]{:S(2)}) collective-permute-start(f32[1,128,128]{2,1,0:T(8,128)S(1)} %get-tuple-element.10), channel_id=1, source_target_pairs={{1,0},{2,1},{3,2},{0,3},{5,4},{6,5},{7,6},{4,7},{9,8},{10,9},{11,1... | collective-permute-start | bytes 196616 | tf_op jit(solution)/shard_map/ppermute | solution.py:20
  670.1 8.5 %collective-permute-start.52 = (f32[1,128,128]{2,1,0:T(8,128)S(1)}, f32[1,128,128]{2,1,0:T(8,128)S(1)}, u32[]{:S(2)}, u32[]{:S(2)}) collective-permute-start(f32[1,128,128]{2,1,0:T(8,128)S(1)} %get-tuple-element.12), channel_id=1, source_target_pairs={{0,1},{1,2},{2,3},{3,0},{4,5},{5,6},{6,7},{7,4},{8,9},{9,10},{10,1... | collective-permute-start | bytes 196616 | tf_op jit(solution)/shard_map/ppermute | solution.py:19
  (115 other events, 1150.8 us)
